TPU v7x, 32 devices: a whole 2x2x4 slice. The times are simulated.
32 devices in a mesh: case: 2 (over y), blk: 4 (over z), freq: 4 (over x, core).
Axes of the slice: x: 2, y: 2, z: 4, core: 2. Of those that a mesh axis runs over, the one named last changes fastest.
Arguments:
- geometry: bfloat16 [3, 8192], P(None, ('case', 'blk')), parts along dimension 1, may hold values from -4 to 4
- modes: bfloat16 [4, 8192, 128], P('freq', ('case', 'blk')), parts along dimension 1, may hold values from -6 to 6
- reduced_freq: float32 [16], replicated, may hold values from 0.1 to 1.5
- freq_index: int32 [8, 3], P(('case', 'freq')), parts along dimension 0, may hold values from 0 to 15
Outputs:
- grad_geometry: float32 [3, 8192], P(None, ('case', 'blk', 'freq')), parts along dimension 1
- forces: float32 [8, 2, 32, 32], P(('case', 'freq')), parts along dimension 0
There are 2 independent parts, one for each index of `case`. A program takes and returns all parts, laid end to end along the dimension named above; an argument that names none is the same for every part. Nothing has to cross between parts.
All inputs are finite; a program needn't handle non-finite values.
Results may differ from a plain program's by a relative error of at most 0.003.
Values may be sent and summed in bfloat16 or wider, within the bound.
No kernel may reach another device: no remote copies, remote signals or barrier semaphores. Data moves between devices by JAX's collectives and lax.ppermute only.
A program may use at most 64 MiB of HBM per device.

v0:
```python
import math
import jax
import jax.numpy as jnp
from jax import lax
from jax.sharding import PartitionSpec as P

CHORD_SHIFT = 0.5
CORE_SQUARE = 0.25


def passed_along(value, axis, steps):
    count = lax.axis_size(axis)
    pairs = [(source, (source + steps) % count) for source in range(count)]
    return lax.ppermute(value, axis, pairs)


def prepare_sender(send_modes):
    columns = send_modes.shape[1] // 4
    flipped = jnp.concatenate([send_modes[:, 2 * columns :], send_modes[:, : 2 * columns]], axis=1)
    turned = jnp.concatenate(
        [
            send_modes[:, 3 * columns :],
            -send_modes[:, 2 * columns : 3 * columns],
            send_modes[:, columns : 2 * columns],
            -send_modes[:, :columns],
        ],
        axis=1,
    )
    paired = jnp.concatenate([flipped, turned], axis=0)
    strength = jnp.concatenate(
        [
            send_modes[:, 2 * columns :],
            jnp.concatenate(
                [-send_modes[:, 3 * columns :], send_modes[:, 2 * columns : 3 * columns]], axis=1
            ),
        ],
        axis=0,
    )
    return (paired, strength)


def block_terms(recv_geom, recv_modes, send_pos, paired, strength, wavenumber):
    send_count = send_pos.shape[1]
    coupled = lax.dot_general(
        recv_modes, paired, (((1,), (1,)), ((), ())), preferred_element_type=jnp.float32
    )
    real_part = coupled[:, :send_count]
    imag_part = coupled[:, send_count:]
    recv_pos = recv_geom.astype(jnp.float32)
    delta_x = recv_pos[0][:, None] + CHORD_SHIFT - send_pos[0][None, :]
    delta_y = recv_pos[1][:, None] - send_pos[1][None, :]
    delta_z = recv_pos[2][:, None] - send_pos[2][None, :]
    inverse = lax.rsqrt(delta_x * delta_x + delta_y * delta_y + delta_z * delta_z + CORE_SQUARE)
    phase = wavenumber * delta_x
    cosine = jnp.cos(phase)
    sine = jnp.sin(phase)
    along = cosine * real_part + sine * imag_part
    across = cosine * imag_part - sine * real_part
    cubed = inverse * inverse * inverse * along
    grad_x = wavenumber * inverse * across - delta_x * cubed
    grad_y = -delta_y * cubed
    grad_z = -delta_z * cubed
    row_grad = jnp.stack([grad_x.sum(axis=1), grad_y.sum(axis=1), grad_z.sum(axis=1)])
    col_grad = -jnp.stack([grad_x.sum(axis=0), grad_y.sum(axis=0), grad_z.sum(axis=0)])
    kernel = jnp.concatenate([cosine * inverse, -sine * inverse], axis=1).astype(jnp.bfloat16)
    pressure = jnp.dot(kernel, strength, preferred_element_type=jnp.float32)
    return (row_grad, col_grad, pressure)


def spread(stacked):
    return lax.psum_scatter(stacked, "freq", scatter_dimension=2, tiled=True)


def local(geometry, modes, reduced_freq, freq_index):
    row_count = geometry.shape[1]
    own_modes = modes[0]
    columns = own_modes.shape[1] // 4
    steps = freq_index.shape[1]
    table_size = reduced_freq.shape[0]
    selected = freq_index[0][:, None] == jnp.arange(table_size, dtype=jnp.int32)[None, :]
    wavenumbers = jnp.sum(jnp.where(selected, reduced_freq[None, :], 0.0), axis=1)
    local_block = (geometry, own_modes)
    sending = [local_block]
    current = local_block
    for offset in range(1, steps):
        current = passed_along((current[0], current[1]), "blk", 1)
        sending.append(current)
    block_rows = min(128, row_count)
    block_count = row_count // block_rows
    recv_geom = geometry.reshape(3, block_count, block_rows).transpose(1, 0, 2)
    recv_modes = own_modes.reshape(block_count, block_rows, 4 * columns)
    row_total = jnp.zeros((3, row_count), jnp.float32)
    pressure_total = jnp.zeros((row_count, 2 * columns), jnp.float32)
    col_parts = []
    for offset in range(steps):
        send_geom, send_modes = sending[offset]
        paired, strength = prepare_sender(send_modes)
        send_pos = send_geom.astype(jnp.float32)
        wavenumber = wavenumbers[offset]

        def visit(
            carry,
            operands,
            send_pos=send_pos,
            paired=paired,
            strength=strength,
            wavenumber=wavenumber,
        ):
            row_grad, col_grad, pressure = block_terms(
                operands[0], operands[1], send_pos, paired, strength, wavenumber
            )
            return (carry + col_grad, (row_grad, pressure))

        col_grad, (row_parts, pressure_parts) = lax.scan(
            visit, jnp.zeros((3, row_count), jnp.float32), (recv_geom, recv_modes)
        )
        row_total = row_total + row_parts.transpose(1, 0, 2).reshape(3, row_count)
        pressure_total = pressure_total + pressure_parts.reshape(row_count, 2 * columns)
        col_parts.append(col_grad)
    local_grad = row_total + col_parts[0]
    grad_scale = 1.0 / math.sqrt(columns * steps * row_count * lax.axis_size("freq"))
    total = local_grad
    for offset in range(1, steps):
        total = total + passed_along(col_parts[offset], "blk", -offset)
    result = spread((total * grad_scale)[None])[0]
    adjoint = own_modes[:, : 2 * columns].astype(jnp.float32)
    adj_real = adjoint[:, :columns]
    adj_imag = adjoint[:, columns:]
    press_real = pressure_total[:, :columns]
    press_imag = pressure_total[:, columns:]
    contract = (((0,), (0,)), ((), ()))
    force_real = lax.dot_general(
        adj_real, press_real, contract, precision=lax.Precision.HIGHEST
    ) + lax.dot_general(adj_imag, press_imag, contract, precision=lax.Precision.HIGHEST)
    force_imag = lax.dot_general(
        adj_real, press_imag, contract, precision=lax.Precision.HIGHEST
    ) - lax.dot_general(adj_imag, press_real, contract, precision=lax.Precision.HIGHEST)
    force_local = jnp.stack([force_real, force_imag])
    force_total = lax.psum(force_local, "blk")
    force_scale = 1.0 / math.sqrt(row_count * row_count * lax.axis_size("blk") * steps)
    return (result, (force_total * force_scale)[None])


def solution(mesh):
    return jax.shard_map(
        local,
        mesh=mesh,
        in_specs=(
            P(None, ("case", "blk")),
            P("freq", ("case", "blk"), None),
            P(),
            P(("case", "freq"), None),
        ),
        out_specs=(P(None, ("case", "blk", "freq")), P(("case", "freq"), None, None, None)),
        check_vma=False,
    )
```

profile of v0, /device:TPU:0, one launch (start us, length us, event | category | flops | bytes accessed | tf_op | source)
XLA Modules:
  0.0 178.1 jit_solution(9225079058068563746)
XLA Ops:
  7.2 3.1 %collective-permute-start.1 = (bf16[1024,128]{1,0:T(8,128)(2,1)}, bf16[1024,128]{1,0:T(8,128)(2,1)S(1)}, u32[]{:S(2)}, u32[]{:S(2)}) collective-permute-start(bf16[1024,128]{1,0:T(8,128)(2,1)} %bitcast.219), channel_id=1, source_target_pairs={{0,4},{4,8},{8,12},{12,0},{1,5},{5,9},{9,13},{13,1},{2,6},{6,10},{... | collective-permute-start | bytes 786440 | tf_op jit(solution)/shard_map/ppermute | solution.py:14
  10.3 1.6 collective-permute-start
  11.9 1.7 slice_negate_fusion.8
  13.7 0.6 copy-done.2
  14.8 0.5 maximum_maximum_fusion
  15.3 0.7 fusion.139
  16.0 3.0 %collective-permute-done = bf16[3,1024]{1,0:T(4,128)(2,1)S(1)} collective-permute-done((bf16[3,1024]{1,0:T(4,128)(2,1)}, bf16[3,1024]{1,0:T(4,128)(2,1)S(1)}, u32[]{:S(2)}, u32[]{:S(2)}) %collective-permute-start) | collective-permute-done | bytes 6176 | tf_op jit(solution)/shard_map/ppermute | solution.py:14
  19.0 34.4 %while.45 = (s32[]{:T(128)}, f32[3,1024]{1,0:T(4,128)S(1)}, f32[8,3,128]{2,1,0:T(4,128)S(1)}, f32[8,128,64]{1,2,0:T(8,128)S(1)}, f32[]{:T(128)}, /*index=5*/bf16...) while((s32[]{:T(128)}, f32[3,1024]{1,0:T(4,128)S(1)}, ...), condition=%wide.region_8.9_spmd.clone, body=%wide.region_1.8_spmd.clone.sunk | while | flops 106967936 | bytes 6464403 | solution.py:114
  19.4 3.2 %fusion.185 = (bf16[128,1024]{1,0:T(8,128)(2,1)S(1)}, bf16[128,1024]{1,0:T(8,128)(2,1)S(1)}, f32[128,1024]{1,0:T(8,128)S(1)}, f32[128,1024]{1,0:T(8,128)S(1)}) fusion(f32[1024]{0:T(1024)S(1)} %bitcast.228, f32[128]{0:T(128)S(1)} %get-tuple-element.645, f32[1024]{0:T(1024)S(1)} %bitcast.230, f32[128]{0:T(128)S(1)} %get-tuple-element.647, ...), kind=kLoop, calls=%fused_computation.25.clone.1 | loop fusion | flops 3670016 | bytes 2635268 | tf_op jit(solution)/shard_map/convert
  23.7 3.2 %fusion.185 = (bf16[128,1024]{1,0:T(8,128)(2,1)S(1)}, bf16[128,1024]{1,0:T(8,128)(2,1)S(1)}, f32[128,1024]{1,0:T(8,128)S(1)}, f32[128,1024]{1,0:T(8,128)S(1)}) fusion(f32[1024]{0:T(1024)S(1)} %bitcast.228, f32[128]{0:T(128)S(1)} %get-tuple-element.645, f32[1024]{0:T(1024)S(1)} %bitcast.230, f32[128]{0:T(128)S(1)} %get-tuple-element.647, ...), kind=kLoop, calls=%fused_computation.25.clone.1 | loop fusion | flops 3670016 | bytes 2635268 | tf_op jit(solution)/shard_map/convert
  27.2 0.4 fusion.186
  28.0 3.2 %fusion.185 = (bf16[128,1024]{1,0:T(8,128)(2,1)S(1)}, bf16[128,1024]{1,0:T(8,128)(2,1)S(1)}, f32[128,1024]{1,0:T(8,128)S(1)}, f32[128,1024]{1,0:T(8,128)S(1)}) fusion(f32[1024]{0:T(1024)S(1)} %bitcast.228, f32[128]{0:T(128)S(1)} %get-tuple-element.645, f32[1024]{0:T(1024)S(1)} %bitcast.230, f32[128]{0:T(128)S(1)} %get-tuple-element.647, ...), kind=kLoop, calls=%fused_computation.25.clone.1 | loop fusion | flops 3670016 | bytes 2635268 | tf_op jit(solution)/shard_map/convert
  32.3 3.2 %fusion.185 = (bf16[128,1024]{1,0:T(8,128)(2,1)S(1)}, bf16[128,1024]{1,0:T(8,128)(2,1)S(1)}, f32[128,1024]{1,0:T(8,128)S(1)}, f32[128,1024]{1,0:T(8,128)S(1)}) fusion(f32[1024]{0:T(1024)S(1)} %bitcast.228, f32[128]{0:T(128)S(1)} %get-tuple-element.645, f32[1024]{0:T(1024)S(1)} %bitcast.230, f32[128]{0:T(128)S(1)} %get-tuple-element.647, ...), kind=kLoop, calls=%fused_computation.25.clone.1 | loop fusion | flops 3670016 | bytes 2635268 | tf_op jit(solution)/shard_map/convert
  36.6 3.2 %fusion.185 = (bf16[128,1024]{1,0:T(8,128)(2,1)S(1)}, bf16[128,1024]{1,0:T(8,128)(2,1)S(1)}, f32[128,1024]{1,0:T(8,128)S(1)}, f32[128,1024]{1,0:T(8,128)S(1)}) fusion(f32[1024]{0:T(1024)S(1)} %bitcast.228, f32[128]{0:T(128)S(1)} %get-tuple-element.645, f32[1024]{0:T(1024)S(1)} %bitcast.230, f32[128]{0:T(128)S(1)} %get-tuple-element.647, ...), kind=kLoop, calls=%fused_computation.25.clone.1 | loop fusion | flops 3670016 | bytes 2635268 | tf_op jit(solution)/shard_map/convert
  40.9 3.2 %fusion.185 = (bf16[128,1024]{1,0:T(8,128)(2,1)S(1)}, bf16[128,1024]{1,0:T(8,128)(2,1)S(1)}, f32[128,1024]{1,0:T(8,128)S(1)}, f32[128,1024]{1,0:T(8,128)S(1)}) fusion(f32[1024]{0:T(1024)S(1)} %bitcast.228, f32[128]{0:T(128)S(1)} %get-tuple-element.645, f32[1024]{0:T(1024)S(1)} %bitcast.230, f32[128]{0:T(128)S(1)} %get-tuple-element.647, ...), kind=kLoop, calls=%fused_computation.25.clone.1 | loop fusion | flops 3670016 | bytes 2635268 | tf_op jit(solution)/shard_map/convert
  44.4 0.4 fusion.186
  45.2 3.2 %fusion.185 = (bf16[128,1024]{1,0:T(8,128)(2,1)S(1)}, bf16[128,1024]{1,0:T(8,128)(2,1)S(1)}, f32[128,1024]{1,0:T(8,128)S(1)}, f32[128,1024]{1,0:T(8,128)S(1)}) fusion(f32[1024]{0:T(1024)S(1)} %bitcast.228, f32[128]{0:T(128)S(1)} %get-tuple-element.645, f32[1024]{0:T(1024)S(1)} %bitcast.230, f32[128]{0:T(128)S(1)} %get-tuple-element.647, ...), kind=kLoop, calls=%fused_computation.25.clone.1 | loop fusion | flops 3670016 | bytes 2635268 | tf_op jit(solution)/shard_map/convert
  49.5 3.2 %fusion.185 = (bf16[128,1024]{1,0:T(8,128)(2,1)S(1)}, bf16[128,1024]{1,0:T(8,128)(2,1)S(1)}, f32[128,1024]{1,0:T(8,128)S(1)}, f32[128,1024]{1,0:T(8,128)S(1)}) fusion(f32[1024]{0:T(1024)S(1)} %bitcast.228, f32[128]{0:T(128)S(1)} %get-tuple-element.645, f32[1024]{0:T(1024)S(1)} %bitcast.230, f32[128]{0:T(128)S(1)} %get-tuple-element.647, ...), kind=kLoop, calls=%fused_computation.25.clone.1 | loop fusion | flops 3670016 | bytes 2635268 | tf_op jit(solution)/shard_map/convert
  53.0 0.4 fusion.186
  54.2 0.5 maximum_maximum_fusion.2
  54.7 1.3 collective-permute-start.3
  56.0 34.7 %while.46 = (s32[]{:T(128)}, f32[3,1024]{1,0:T(4,128)S(1)}, f32[8,3,128]{2,1,0:T(4,128)S(1)}, f32[8,128,64]{1,2,0:T(8,128)S(1)}, f32[]{:T(128)}, /*index=5*/bf16...) while((s32[]{:T(128)}, f32[3,1024]{1,0:T(4,128)S(1)}, ...), condition=%wide.region_16.17_spmd.clone, body=%wide.region_9.16_spmd.clone.sunk | while | flops 106967936 | bytes 6464403 | solution.py:114
  56.4 3.2 %fusion.196 = (bf16[128,1024]{1,0:T(8,128)(2,1)S(1)}, bf16[128,1024]{1,0:T(8,128)(2,1)S(1)}, f32[128,1024]{1,0:T(8,128)S(1)}, f32[128,1024]{1,0:T(8,128)S(1)}) fusion(f32[1024]{0:T(1024)S(1)} %bitcast.232, f32[128]{0:T(128)S(1)} %get-tuple-element.671, f32[1024]{0:T(1024)S(1)} %bitcast.234, f32[128]{0:T(128)S(1)} %get-tuple-element.673, ...), kind=kLoop, calls=%fused_computation.77.clone.1 | loop fusion | flops 3670016 | bytes 2635268 | tf_op jit(solution)/shard_map/convert.2
  60.8 3.2 %fusion.196 = (bf16[128,1024]{1,0:T(8,128)(2,1)S(1)}, bf16[128,1024]{1,0:T(8,128)(2,1)S(1)}, f32[128,1024]{1,0:T(8,128)S(1)}, f32[128,1024]{1,0:T(8,128)S(1)}) fusion(f32[1024]{0:T(1024)S(1)} %bitcast.232, f32[128]{0:T(128)S(1)} %get-tuple-element.671, f32[1024]{0:T(1024)S(1)} %bitcast.234, f32[128]{0:T(128)S(1)} %get-tuple-element.673, ...), kind=kLoop, calls=%fused_computation.77.clone.1 | loop fusion | flops 3670016 | bytes 2635268 | tf_op jit(solution)/shard_map/convert.2
  65.1 3.2 %fusion.196 = (bf16[128,1024]{1,0:T(8,128)(2,1)S(1)}, bf16[128,1024]{1,0:T(8,128)(2,1)S(1)}, f32[128,1024]{1,0:T(8,128)S(1)}, f32[128,1024]{1,0:T(8,128)S(1)}) fusion(f32[1024]{0:T(1024)S(1)} %bitcast.232, f32[128]{0:T(128)S(1)} %get-tuple-element.671, f32[1024]{0:T(1024)S(1)} %bitcast.234, f32[128]{0:T(128)S(1)} %get-tuple-element.673, ...), kind=kLoop, calls=%fused_computation.77.clone.1 | loop fusion | flops 3670016 | bytes 2635268 | tf_op jit(solution)/shard_map/convert.2
  69.4 3.2 %fusion.196 = (bf16[128,1024]{1,0:T(8,128)(2,1)S(1)}, bf16[128,1024]{1,0:T(8,128)(2,1)S(1)}, f32[128,1024]{1,0:T(8,128)S(1)}, f32[128,1024]{1,0:T(8,128)S(1)}) fusion(f32[1024]{0:T(1024)S(1)} %bitcast.232, f32[128]{0:T(128)S(1)} %get-tuple-element.671, f32[1024]{0:T(1024)S(1)} %bitcast.234, f32[128]{0:T(128)S(1)} %get-tuple-element.673, ...), kind=kLoop, calls=%fused_computation.77.clone.1 | loop fusion | flops 3670016 | bytes 2635268 | tf_op jit(solution)/shard_map/convert.2
  73.8 3.2 %fusion.196 = (bf16[128,1024]{1,0:T(8,128)(2,1)S(1)}, bf16[128,1024]{1,0:T(8,128)(2,1)S(1)}, f32[128,1024]{1,0:T(8,128)S(1)}, f32[128,1024]{1,0:T(8,128)S(1)}) fusion(f32[1024]{0:T(1024)S(1)} %bitcast.232, f32[128]{0:T(128)S(1)} %get-tuple-element.671, f32[1024]{0:T(1024)S(1)} %bitcast.234, f32[128]{0:T(128)S(1)} %get-tuple-element.673, ...), kind=kLoop, calls=%fused_computation.77.clone.1 | loop fusion | flops 3670016 | bytes 2635268 | tf_op jit(solution)/shard_map/convert.2
  78.1 3.2 %fusion.196 = (bf16[128,1024]{1,0:T(8,128)(2,1)S(1)}, bf16[128,1024]{1,0:T(8,128)(2,1)S(1)}, f32[128,1024]{1,0:T(8,128)S(1)}, f32[128,1024]{1,0:T(8,128)S(1)}) fusion(f32[1024]{0:T(1024)S(1)} %bitcast.232, f32[128]{0:T(128)S(1)} %get-tuple-element.671, f32[1024]{0:T(1024)S(1)} %bitcast.234, f32[128]{0:T(128)S(1)} %get-tuple-element.673, ...), kind=kLoop, calls=%fused_computation.77.clone.1 | loop fusion | flops 3670016 | bytes 2635268 | tf_op jit(solution)/shard_map/convert.2
  82.5 3.2 %fusion.196 = (bf16[128,1024]{1,0:T(8,128)(2,1)S(1)}, bf16[128,1024]{1,0:T(8,128)(2,1)S(1)}, f32[128,1024]{1,0:T(8,128)S(1)}, f32[128,1024]{1,0:T(8,128)S(1)}) fusion(f32[1024]{0:T(1024)S(1)} %bitcast.232, f32[128]{0:T(128)S(1)} %get-tuple-element.671, f32[1024]{0:T(1024)S(1)} %bitcast.234, f32[128]{0:T(128)S(1)} %get-tuple-element.673, ...), kind=kLoop, calls=%fused_computation.77.clone.1 | loop fusion | flops 3670016 | bytes 2635268 | tf_op jit(solution)/shard_map/convert.2
  86.8 3.2 %fusion.196 = (bf16[128,1024]{1,0:T(8,128)(2,1)S(1)}, bf16[128,1024]{1,0:T(8,128)(2,1)S(1)}, f32[128,1024]{1,0:T(8,128)S(1)}, f32[128,1024]{1,0:T(8,128)S(1)}) fusion(f32[1024]{0:T(1024)S(1)} %bitcast.232, f32[128]{0:T(128)S(1)} %get-tuple-element.671, f32[1024]{0:T(1024)S(1)} %bitcast.234, f32[128]{0:T(128)S(1)} %get-tuple-element.673, ...), kind=kLoop, calls=%fused_computation.77.clone.1 | loop fusion | flops 3670016 | bytes 2635268 | tf_op jit(solution)/shard_map/convert.2
  90.8 2.6 %collective-permute-start.4 = (f32[3,1024]{1,0:T(4,128)S(1)}, f32[3,1024]{1,0:T(4,128)S(1)}, u32[]{:S(2)}, u32[]{:S(2)}) collective-permute-start(f32[3,1024]{1,0:T(4,128)S(1)} %get-tuple-element.168), channel_id=1, source_target_pairs={{0,12},{4,0},{8,4},{12,8},{1,13},{5,1},{9,5},{13,9},{2,14},{6,2},{... | collective-permute-start | bytes 36872 | tf_op jit(solution)/shard_map/ppermute | solution.py:14
  94.0 0.5 maximum_maximum_fusion.4
  94.6 34.4 %while.47 = (s32[]{:T(128)}, f32[3,1024]{1,0:T(4,128)S(1)}, f32[8,3,128]{2,1,0:T(4,128)S(1)}, f32[8,128,64]{1,2,0:T(8,128)S(1)}, f32[]{:T(128)}, /*index=5*/bf16...) while((s32[]{:T(128)}, f32[3,1024]{1,0:T(4,128)S(1)}, ...), condition=%wide.region_24.25_spmd.clone, body=%wide.region_17.24_spmd.clone.sunk | while | flops 106967936 | bytes 6464403 | solution.py:114
  94.9 3.2 %fusion.207 = (bf16[128,1024]{1,0:T(8,128)(2,1)S(1)}, bf16[128,1024]{1,0:T(8,128)(2,1)S(1)}, f32[128,1024]{1,0:T(8,128)S(1)}, f32[128,1024]{1,0:T(8,128)S(1)}) fusion(f32[1024]{0:T(1024)S(1)} %bitcast.236, f32[128]{0:T(128)S(1)} %get-tuple-element.697, f32[1024]{0:T(1024)S(1)} %bitcast.238, f32[128]{0:T(128)S(1)} %get-tuple-element.699, ...), kind=kLoop, calls=%fused_computation.129.clone.1 | loop fusion | flops 3670016 | bytes 2635268 | tf_op jit(solution)/shard_map/convert.4
  99.2 3.2 %fusion.207 = (bf16[128,1024]{1,0:T(8,128)(2,1)S(1)}, bf16[128,1024]{1,0:T(8,128)(2,1)S(1)}, f32[128,1024]{1,0:T(8,128)S(1)}, f32[128,1024]{1,0:T(8,128)S(1)}) fusion(f32[1024]{0:T(1024)S(1)} %bitcast.236, f32[128]{0:T(128)S(1)} %get-tuple-element.697, f32[1024]{0:T(1024)S(1)} %bitcast.238, f32[128]{0:T(128)S(1)} %get-tuple-element.699, ...), kind=kLoop, calls=%fused_computation.129.clone.1 | loop fusion | flops 3670016 | bytes 2635268 | tf_op jit(solution)/shard_map/convert.4
  103.5 3.2 %fusion.207 = (bf16[128,1024]{1,0:T(8,128)(2,1)S(1)}, bf16[128,1024]{1,0:T(8,128)(2,1)S(1)}, f32[128,1024]{1,0:T(8,128)S(1)}, f32[128,1024]{1,0:T(8,128)S(1)}) fusion(f32[1024]{0:T(1024)S(1)} %bitcast.236, f32[128]{0:T(128)S(1)} %get-tuple-element.697, f32[1024]{0:T(1024)S(1)} %bitcast.238, f32[128]{0:T(128)S(1)} %get-tuple-element.699, ...), kind=kLoop, calls=%fused_computation.129.clone.1 | loop fusion | flops 3670016 | bytes 2635268 | tf_op jit(solution)/shard_map/convert.4
  107.8 3.2 %fusion.207 = (bf16[128,1024]{1,0:T(8,128)(2,1)S(1)}, bf16[128,1024]{1,0:T(8,128)(2,1)S(1)}, f32[128,1024]{1,0:T(8,128)S(1)}, f32[128,1024]{1,0:T(8,128)S(1)}) fusion(f32[1024]{0:T(1024)S(1)} %bitcast.236, f32[128]{0:T(128)S(1)} %get-tuple-element.697, f32[1024]{0:T(1024)S(1)} %bitcast.238, f32[128]{0:T(128)S(1)} %get-tuple-element.699, ...), kind=kLoop, calls=%fused_computation.129.clone.1 | loop fusion | flops 3670016 | bytes 2635268 | tf_op jit(solution)/shard_map/convert.4
  112.2 3.2 %fusion.207 = (bf16[128,1024]{1,0:T(8,128)(2,1)S(1)}, bf16[128,1024]{1,0:T(8,128)(2,1)S(1)}, f32[128,1024]{1,0:T(8,128)S(1)}, f32[128,1024]{1,0:T(8,128)S(1)}) fusion(f32[1024]{0:T(1024)S(1)} %bitcast.236, f32[128]{0:T(128)S(1)} %get-tuple-element.697, f32[1024]{0:T(1024)S(1)} %bitcast.238, f32[128]{0:T(128)S(1)} %get-tuple-element.699, ...), kind=kLoop, calls=%fused_computation.129.clone.1 | loop fusion | flops 3670016 | bytes 2635268 | tf_op jit(solution)/shard_map/convert.4
  116.5 3.2 %fusion.207 = (bf16[128,1024]{1,0:T(8,128)(2,1)S(1)}, bf16[128,1024]{1,0:T(8,128)(2,1)S(1)}, f32[128,1024]{1,0:T(8,128)S(1)}, f32[128,1024]{1,0:T(8,128)S(1)}) fusion(f32[1024]{0:T(1024)S(1)} %bitcast.236, f32[128]{0:T(128)S(1)} %get-tuple-element.697, f32[1024]{0:T(1024)S(1)} %bitcast.238, f32[128]{0:T(128)S(1)} %get-tuple-element.699, ...), kind=kLoop, calls=%fused_computation.129.clone.1 | loop fusion | flops 3670016 | bytes 2635268 | tf_op jit(solution)/shard_map/convert.4
  120.8 3.2 %fusion.207 = (bf16[128,1024]{1,0:T(8,128)(2,1)S(1)}, bf16[128,1024]{1,0:T(8,128)(2,1)S(1)}, f32[128,1024]{1,0:T(8,128)S(1)}, f32[128,1024]{1,0:T(8,128)S(1)}) fusion(f32[1024]{0:T(1024)S(1)} %bitcast.236, f32[128]{0:T(128)S(1)} %get-tuple-element.697, f32[1024]{0:T(1024)S(1)} %bitcast.238, f32[128]{0:T(128)S(1)} %get-tuple-element.699, ...), kind=kLoop, calls=%fused_computation.129.clone.1 | loop fusion | flops 3670016 | bytes 2635268 | tf_op jit(solution)/shard_map/convert.4
  125.1 3.2 %fusion.207 = (bf16[128,1024]{1,0:T(8,128)(2,1)S(1)}, bf16[128,1024]{1,0:T(8,128)(2,1)S(1)}, f32[128,1024]{1,0:T(8,128)S(1)}, f32[128,1024]{1,0:T(8,128)S(1)}) fusion(f32[1024]{0:T(1024)S(1)} %bitcast.236, f32[128]{0:T(128)S(1)} %get-tuple-element.697, f32[1024]{0:T(1024)S(1)} %bitcast.238, f32[128]{0:T(128)S(1)} %get-tuple-element.699, ...), kind=kLoop, calls=%fused_computation.129.clone.1 | loop fusion | flops 3670016 | bytes 2635268 | tf_op jit(solution)/shard_map/convert.4
  128.6 0.4 fusion.208
  130.2 0.6 collective-permute-start.5
  130.8 17.7 %psum.7 = f32[2,32,32]{1,2,0:T(8,128)S(1)} all-reduce(f32[2,32,32]{1,2,0:T(8,128)S(1)} %pad_maximum_fusion), channel_id=1, replica_groups=mesh['case'=2,'blk'=4,'freq'=4] {'blk'}, use_global_device_ids=true, to_apply=%region_26.27 | all-reduce | flops 2048 | bytes 16384 | tf_op jit(solution)/shard_map/psum | solution.py:139
  148.6 1.0 copy.13
  149.7 0.7 copy.12
  150.4 19.2 %reduce-scatter.4.cloned.1.call-done = f32[256,3]{1,0:T(8,128)} async-done(((f32[1024,3]{1,0:T(8,128)}), f32[256,3]{1,0:T(8,128)}) %reduce-scatter.4.cloned.1.call-update) | async-done | bytes 3088
  169.6 1.6 copy.14
  (232 shorter events, 27.6 us)
Async XLA Ops:
  7.2 162.5 %reduce-scatter.4.cloned.1.call-start = ((), (), s32[]{:S(2)}) async-start(), calls=%async_computation.1 | async-start | bytes 655360
  7.2 46.3 %collective-permute-start.1 = (bf16[1024,128]{1,0:T(8,128)(2,1)}, bf16[1024,128]{1,0:T(8,128)(2,1)S(1)}, u32[]{:S(2)}, u32[]{:S(2)}) collective-permute-start(bf16[1024,128]{1,0:T(8,128)(2,1)} %bitcast.219), channel_id=1, source_target_pairs={{0,4},{4,8},{8,12},{12,0},{1,5},{5,9},{9,13},{13,1},{2,6},{6,10},{... | collective-permute-start | bytes 786440 | tf_op jit(solution)/shard_map/ppermute | solution.py:14
  10.3 8.7 %collective-permute-start = (bf16[3,1024]{1,0:T(4,128)(2,1)}, bf16[3,1024]{1,0:T(4,128)(2,1)S(1)}, u32[]{:S(2)}, u32[]{:S(2)}) collective-permute-start(bf16[3,1024]{1,0:T(4,128)(2,1)} %param.10), channel_id=1, source_target_pairs={{0,4},{4,8},{8,12},{12,0},{1,5},{5,9},{9,13},{13,1},{2,6},{6,10},{... | collective-permute-start | bytes 18440 | tf_op jit(solution)/shard_map/ppermute | solution.py:14
  11.9 1.7 copy-start
  13.7 0.7 copy-start.2
  13.7 0.7 copy-start.3
  14.8 1.2 copy-start.1
  19.0 34.5 %collective-permute-start.2 = (bf16[3,1024]{1,0:T(4,128)(2,1)S(1)}, bf16[3,1024]{1,0:T(4,128)(2,1)S(1)}, u32[]{:S(2)}, u32[]{:S(2)}) collective-permute-start(bf16[3,1024]{1,0:T(4,128)(2,1)S(1)} %collective-permute-done), channel_id=1, source_target_pairs={{0,4},{4,8},{8,12},{12,0},{1,5},{5,9},{9,13},{13,1},{2,6},{6,10},{... | collective-permute-start | bytes 18440 | tf_op jit(solution)/shard_map/ppermute | solution.py:14
  54.7 38.7 %collective-permute-start.3 = (bf16[1024,128]{1,0:T(8,128)(2,1)S(1)}, bf16[1024,128]{1,0:T(8,128)(2,1)S(1)}, u32[]{:S(2)}, u32[]{:S(2)}) collective-permute-start(bf16[1024,128]{1,0:T(8,128)(2,1)S(1)} %collective-permute-done.1), channel_id=1, source_target_pairs={{0,4},{4,8},{8,12},{12,0},{1,5},{5,9},{9,13},{13,1},{2,6},{6,10},{... | collective-permute-start | bytes 786440 | tf_op jit(solution)/shard_map/ppermute | solution.py:14
  90.8 57.8 %collective-permute-start.4 = (f32[3,1024]{1,0:T(4,128)S(1)}, f32[3,1024]{1,0:T(4,128)S(1)}, u32[]{:S(2)}, u32[]{:S(2)}) collective-permute-start(f32[3,1024]{1,0:T(4,128)S(1)} %get-tuple-element.168), channel_id=1, source_target_pairs={{0,12},{4,0},{8,4},{12,8},{1,13},{5,1},{9,5},{13,9},{2,14},{6,2},{... | collective-permute-start | bytes 36872 | tf_op jit(solution)/shard_map/ppermute | solution.py:14
  130.2 18.4 %collective-permute-start.5 = (f32[3,1024]{1,0:T(4,128)S(1)}, f32[3,1024]{1,0:T(4,128)S(1)}, u32[]{:S(2)}, u32[]{:S(2)}) collective-permute-start(f32[3,1024]{1,0:T(4,128)S(1)} %get-tuple-element.169), channel_id=1, source_target_pairs={{0,8},{4,12},{8,0},{12,4},{1,9},{5,13},{9,1},{13,5},{2,10},{6,14},... | collective-permute-start | bytes 36872 | tf_op jit(solution)/shard_map/ppermute | solution.py:14
Sparse Core Ops, SparseCore 0:
  149.8 19.7 reduce-scatter.3
where the time goes:
time: 178 us
  other arithmetic  91.4 us (51%)
  waiting for transfers between devices  22.3 us (13%)
  blocking collectives  17.7 us (10%)
  matrix products  16.2 us (9%)
  between operations  14.3 us (8%)
  starting transfers between devices  9.26 us (5%)
  local copies, waits for them, and re-layouts  5.38 us (3%)
    another operation x24, other arithmetic  76.2 us
    unnamed x2, waiting for transfers between devices  19.3 us
    psum x1, blocking collectives, local(): force_total = lax.psum(force_local, 'blk')  17.7 us
    ppermute x6, starting transfers between devices, passed_along(): return lax.ppermute(value, axis, pairs)  9.23 us
    reduce_sum x24, other arithmetic, block_terms(): grad_y.sum(axis=1)  9.08 us
    dot_general x24, matrix products, block_terms(): pressure = jnp.dot(kernel, strength, preferred_element_type=jnp.float32)  7.89 us
    dot_general x24, matrix products, block_terms(): lax.dot_general(recv_modes, paired, (((1,), (1,)), ((), ())), preferred_e...  7.17 us
    unnamed x11, local copies, waits for them, and re-layouts  3.97 us
  transfers between devices with their start and end apart: 7, of which 2 were waited for; matrix products, arithmetic and copies ran while one was open for 61% of the time, Pallas kernels for 0%

commit v1 on v0

--- a/solution.py
+++ b/solution.py
@@ -136,7 +136,7 @@
         adj_real, press_imag, contract, precision=lax.Precision.HIGHEST
     ) - lax.dot_general(adj_imag, press_real, contract, precision=lax.Precision.HIGHEST)
     force_local = jnp.stack([force_real, force_imag])
-    force_total = lax.psum(force_local, "blk")
+    force_total = jnp.sum(lax.all_gather(force_local, "blk"), axis=0)
     force_scale = 1.0 / math.sqrt(row_count * row_count * lax.axis_size("blk") * steps)
     return (result, (force_total * force_scale)[None])
 

time: 178 us -> 176 us (0.989)
  blocking collectives: 17.7 us -> 13.6 us
    psum x1 -> x0, blocking collectives: 17.7 us -> none  [local(): force_total = lax.psum(force_local, 'blk')]
    all_gather x0 -> x1, blocking collectives: none -> 13.6 us  [local(): force_total = jnp.sum(lax.all_gather(force_local, 'blk'), axis=0)]
    unnamed x11 -> x12, local copies, waits for them, and re-layouts: 3.97 us -> 4.04 us
  transfers between devices with their start and end apart: 7 -> 7, of which waited for: 2 -> 2; matrix products, arithmetic and copies ran while one was open for 61% -> 62% of each run, Pallas kernels for 0% -> 0%
where the time goes in v1:
time: 176 us; the launch traced here: 175 us
  other arithmetic  91.5 us (52%)
  waiting for transfers between devices  23.7 us (13%)
  matrix products  16.2 us (9%)
  between operations  14.3 us (8%)
  blocking collectives  13.6 us (8%)
  starting transfers between devices  9.21 us (5%)
  local copies, waits for them, and re-layouts  5.53 us (3%)
    another operation x24, other arithmetic  76.2 us
    unnamed x2, waiting for transfers between devices  20.6 us
    all_gather x1, blocking collectives, local(): force_total = jnp.sum(lax.all_gather(force_local, 'blk'), axis=0)  13.6 us
    ppermute x6, starting transfers between devices, passed_along(): return lax.ppermute(value, axis, pairs)  9.17 us
    reduce_sum x24, other arithmetic, block_terms(): grad_y.sum(axis=1)  9.08 us
    dot_general x24, matrix products, block_terms(): pressure = jnp.dot(kernel, strength, preferred_element_type=jnp.float32)  7.89 us
    dot_general x24, matrix products, block_terms(): lax.dot_general(recv_modes, paired, (((1,), (1,)), ((), ())), preferred_e...  7.17 us
    unnamed x12, local copies, waits for them, and re-layouts  4.04 us
  transfers between devices with their start and end apart: 7, of which 2 were waited for; matrix products, arithmetic and copies ran while one was open for 62% of the time, Pallas kernels for 0%

profile of v1, /device:TPU:0, one launch (start us, length us, event | category | flops | bytes accessed | tf_op | source)
XLA Modules:
  0.0 175.4 jit_solution(17995739353087892729)
XLA Ops:
  7.2 3.1 %collective-permute-start.1 = (bf16[1024,128]{1,0:T(8,128)(2,1)}, bf16[1024,128]{1,0:T(8,128)(2,1)S(1)}, u32[]{:S(2)}, u32[]{:S(2)}) collective-permute-start(bf16[1024,128]{1,0:T(8,128)(2,1)} %bitcast.220), channel_id=1, source_target_pairs={{0,4},{4,8},{8,12},{12,0},{1,5},{5,9},{9,13},{13,1},{2,6},{6,10},{... | collective-permute-start | bytes 786440 | tf_op jit(solution)/shard_map/ppermute | solution.py:14
  10.3 1.6 collective-permute-start
  11.9 1.7 slice_negate_fusion.8
  13.7 0.6 copy-done.2
  14.8 0.5 maximum_maximum_fusion
  15.3 0.7 fusion.139
  16.0 3.0 %collective-permute-done = bf16[3,1024]{1,0:T(4,128)(2,1)S(1)} collective-permute-done((bf16[3,1024]{1,0:T(4,128)(2,1)}, bf16[3,1024]{1,0:T(4,128)(2,1)S(1)}, u32[]{:S(2)}, u32[]{:S(2)}) %collective-permute-start) | collective-permute-done | bytes 6176 | tf_op jit(solution)/shard_map/ppermute | solution.py:14
  19.0 34.4 %while.45 = (s32[]{:T(128)}, f32[3,1024]{1,0:T(4,128)S(1)}, f32[8,3,128]{2,1,0:T(4,128)S(1)}, f32[8,128,64]{1,2,0:T(8,128)S(1)}, f32[]{:T(128)}, /*index=5*/bf16...) while((s32[]{:T(128)}, f32[3,1024]{1,0:T(4,128)S(1)}, ...), condition=%wide.region_8.9_spmd.clone, body=%wide.region_1.8_spmd.clone.sunk | while | flops 106967936 | bytes 6464403 | solution.py:114
  19.4 3.2 %fusion.185 = (bf16[128,1024]{1,0:T(8,128)(2,1)S(1)}, bf16[128,1024]{1,0:T(8,128)(2,1)S(1)}, f32[128,1024]{1,0:T(8,128)S(1)}, f32[128,1024]{1,0:T(8,128)S(1)}) fusion(f32[1024]{0:T(1024)S(1)} %bitcast.229, f32[128]{0:T(128)S(1)} %get-tuple-element.641, f32[1024]{0:T(1024)S(1)} %bitcast.231, f32[128]{0:T(128)S(1)} %get-tuple-element.643, ...), kind=kLoop, calls=%fused_computation.25.clone.1 | loop fusion | flops 3670016 | bytes 2635268 | tf_op jit(solution)/shard_map/convert
  23.7 3.2 %fusion.185 = (bf16[128,1024]{1,0:T(8,128)(2,1)S(1)}, bf16[128,1024]{1,0:T(8,128)(2,1)S(1)}, f32[128,1024]{1,0:T(8,128)S(1)}, f32[128,1024]{1,0:T(8,128)S(1)}) fusion(f32[1024]{0:T(1024)S(1)} %bitcast.229, f32[128]{0:T(128)S(1)} %get-tuple-element.641, f32[1024]{0:T(1024)S(1)} %bitcast.231, f32[128]{0:T(128)S(1)} %get-tuple-element.643, ...), kind=kLoop, calls=%fused_computation.25.clone.1 | loop fusion | flops 3670016 | bytes 2635268 | tf_op jit(solution)/shard_map/convert
  27.2 0.4 fusion.186
  28.0 3.2 %fusion.185 = (bf16[128,1024]{1,0:T(8,128)(2,1)S(1)}, bf16[128,1024]{1,0:T(8,128)(2,1)S(1)}, f32[128,1024]{1,0:T(8,128)S(1)}, f32[128,1024]{1,0:T(8,128)S(1)}) fusion(f32[1024]{0:T(1024)S(1)} %bitcast.229, f32[128]{0:T(128)S(1)} %get-tuple-element.641, f32[1024]{0:T(1024)S(1)} %bitcast.231, f32[128]{0:T(128)S(1)} %get-tuple-element.643, ...), kind=kLoop, calls=%fused_computation.25.clone.1 | loop fusion | flops 3670016 | bytes 2635268 | tf_op jit(solution)/shard_map/convert
  32.3 3.2 %fusion.185 = (bf16[128,1024]{1,0:T(8,128)(2,1)S(1)}, bf16[128,1024]{1,0:T(8,128)(2,1)S(1)}, f32[128,1024]{1,0:T(8,128)S(1)}, f32[128,1024]{1,0:T(8,128)S(1)}) fusion(f32[1024]{0:T(1024)S(1)} %bitcast.229, f32[128]{0:T(128)S(1)} %get-tuple-element.641, f32[1024]{0:T(1024)S(1)} %bitcast.231, f32[128]{0:T(128)S(1)} %get-tuple-element.643, ...), kind=kLoop, calls=%fused_computation.25.clone.1 | loop fusion | flops 3670016 | bytes 2635268 | tf_op jit(solution)/shard_map/convert
  36.6 3.2 %fusion.185 = (bf16[128,1024]{1,0:T(8,128)(2,1)S(1)}, bf16[128,1024]{1,0:T(8,128)(2,1)S(1)}, f32[128,1024]{1,0:T(8,128)S(1)}, f32[128,1024]{1,0:T(8,128)S(1)}) fusion(f32[1024]{0:T(1024)S(1)} %bitcast.229, f32[128]{0:T(128)S(1)} %get-tuple-element.641, f32[1024]{0:T(1024)S(1)} %bitcast.231, f32[128]{0:T(128)S(1)} %get-tuple-element.643, ...), kind=kLoop, calls=%fused_computation.25.clone.1 | loop fusion | flops 3670016 | bytes 2635268 | tf_op jit(solution)/shard_map/convert
  40.9 3.2 %fusion.185 = (bf16[128,1024]{1,0:T(8,128)(2,1)S(1)}, bf16[128,1024]{1,0:T(8,128)(2,1)S(1)}, f32[128,1024]{1,0:T(8,128)S(1)}, f32[128,1024]{1,0:T(8,128)S(1)}) fusion(f32[1024]{0:T(1024)S(1)} %bitcast.229, f32[128]{0:T(128)S(1)} %get-tuple-element.641, f32[1024]{0:T(1024)S(1)} %bitcast.231, f32[128]{0:T(128)S(1)} %get-tuple-element.643, ...), kind=kLoop, calls=%fused_computation.25.clone.1 | loop fusion | flops 3670016 | bytes 2635268 | tf_op jit(solution)/shard_map/convert
  44.4 0.4 fusion.186
  45.2 3.2 %fusion.185 = (bf16[128,1024]{1,0:T(8,128)(2,1)S(1)}, bf16[128,1024]{1,0:T(8,128)(2,1)S(1)}, f32[128,1024]{1,0:T(8,128)S(1)}, f32[128,1024]{1,0:T(8,128)S(1)}) fusion(f32[1024]{0:T(1024)S(1)} %bitcast.229, f32[128]{0:T(128)S(1)} %get-tuple-element.641, f32[1024]{0:T(1024)S(1)} %bitcast.231, f32[128]{0:T(128)S(1)} %get-tuple-element.643, ...), kind=kLoop, calls=%fused_computation.25.clone.1 | loop fusion | flops 3670016 | bytes 2635268 | tf_op jit(solution)/shard_map/convert
  49.5 3.2 %fusion.185 = (bf16[128,1024]{1,0:T(8,128)(2,1)S(1)}, bf16[128,1024]{1,0:T(8,128)(2,1)S(1)}, f32[128,1024]{1,0:T(8,128)S(1)}, f32[128,1024]{1,0:T(8,128)S(1)}) fusion(f32[1024]{0:T(1024)S(1)} %bitcast.229, f32[128]{0:T(128)S(1)} %get-tuple-element.641, f32[1024]{0:T(1024)S(1)} %bitcast.231, f32[128]{0:T(128)S(1)} %get-tuple-element.643, ...), kind=kLoop, calls=%fused_computation.25.clone.1 | loop fusion | flops 3670016 | bytes 2635268 | tf_op jit(solution)/shard_map/convert
  53.0 0.4 fusion.186
  54.2 0.5 maximum_maximum_fusion.2
  54.7 1.3 collective-permute-start.3
  56.0 34.7 %while.46 = (s32[]{:T(128)}, f32[3,1024]{1,0:T(4,128)S(1)}, f32[8,3,128]{2,1,0:T(4,128)S(1)}, f32[8,128,64]{1,2,0:T(8,128)S(1)}, f32[]{:T(128)}, /*index=5*/bf16...) while((s32[]{:T(128)}, f32[3,1024]{1,0:T(4,128)S(1)}, ...), condition=%wide.region_16.17_spmd.clone, body=%wide.region_9.16_spmd.clone.sunk | while | flops 106967936 | bytes 6464403 | solution.py:114
  56.4 3.2 %fusion.196 = (bf16[128,1024]{1,0:T(8,128)(2,1)S(1)}, bf16[128,1024]{1,0:T(8,128)(2,1)S(1)}, f32[128,1024]{1,0:T(8,128)S(1)}, f32[128,1024]{1,0:T(8,128)S(1)}) fusion(f32[1024]{0:T(1024)S(1)} %bitcast.233, f32[128]{0:T(128)S(1)} %get-tuple-element.667, f32[1024]{0:T(1024)S(1)} %bitcast.235, f32[128]{0:T(128)S(1)} %get-tuple-element.669, ...), kind=kLoop, calls=%fused_computation.77.clone.1 | loop fusion | flops 3670016 | bytes 2635268 | tf_op jit(solution)/shard_map/convert.2
  60.8 3.2 %fusion.196 = (bf16[128,1024]{1,0:T(8,128)(2,1)S(1)}, bf16[128,1024]{1,0:T(8,128)(2,1)S(1)}, f32[128,1024]{1,0:T(8,128)S(1)}, f32[128,1024]{1,0:T(8,128)S(1)}) fusion(f32[1024]{0:T(1024)S(1)} %bitcast.233, f32[128]{0:T(128)S(1)} %get-tuple-element.667, f32[1024]{0:T(1024)S(1)} %bitcast.235, f32[128]{0:T(128)S(1)} %get-tuple-element.669, ...), kind=kLoop, calls=%fused_computation.77.clone.1 | loop fusion | flops 3670016 | bytes 2635268 | tf_op jit(solution)/shard_map/convert.2
  65.1 3.2 %fusion.196 = (bf16[128,1024]{1,0:T(8,128)(2,1)S(1)}, bf16[128,1024]{1,0:T(8,128)(2,1)S(1)}, f32[128,1024]{1,0:T(8,128)S(1)}, f32[128,1024]{1,0:T(8,128)S(1)}) fusion(f32[1024]{0:T(1024)S(1)} %bitcast.233, f32[128]{0:T(128)S(1)} %get-tuple-element.667, f32[1024]{0:T(1024)S(1)} %bitcast.235, f32[128]{0:T(128)S(1)} %get-tuple-element.669, ...), kind=kLoop, calls=%fused_computation.77.clone.1 | loop fusion | flops 3670016 | bytes 2635268 | tf_op jit(solution)/shard_map/convert.2
  69.4 3.2 %fusion.196 = (bf16[128,1024]{1,0:T(8,128)(2,1)S(1)}, bf16[128,1024]{1,0:T(8,128)(2,1)S(1)}, f32[128,1024]{1,0:T(8,128)S(1)}, f32[128,1024]{1,0:T(8,128)S(1)}) fusion(f32[1024]{0:T(1024)S(1)} %bitcast.233, f32[128]{0:T(128)S(1)} %get-tuple-element.667, f32[1024]{0:T(1024)S(1)} %bitcast.235, f32[128]{0:T(128)S(1)} %get-tuple-element.669, ...), kind=kLoop, calls=%fused_computation.77.clone.1 | loop fusion | flops 3670016 | bytes 2635268 | tf_op jit(solution)/shard_map/convert.2
  73.8 3.2 %fusion.196 = (bf16[128,1024]{1,0:T(8,128)(2,1)S(1)}, bf16[128,1024]{1,0:T(8,128)(2,1)S(1)}, f32[128,1024]{1,0:T(8,128)S(1)}, f32[128,1024]{1,0:T(8,128)S(1)}) fusion(f32[1024]{0:T(1024)S(1)} %bitcast.233, f32[128]{0:T(128)S(1)} %get-tuple-element.667, f32[1024]{0:T(1024)S(1)} %bitcast.235, f32[128]{0:T(128)S(1)} %get-tuple-element.669, ...), kind=kLoop, calls=%fused_computation.77.clone.1 | loop fusion | flops 3670016 | bytes 2635268 | tf_op jit(solution)/shard_map/convert.2
  78.1 3.2 %fusion.196 = (bf16[128,1024]{1,0:T(8,128)(2,1)S(1)}, bf16[128,1024]{1,0:T(8,128)(2,1)S(1)}, f32[128,1024]{1,0:T(8,128)S(1)}, f32[128,1024]{1,0:T(8,128)S(1)}) fusion(f32[1024]{0:T(1024)S(1)} %bitcast.233, f32[128]{0:T(128)S(1)} %get-tuple-element.667, f32[1024]{0:T(1024)S(1)} %bitcast.235, f32[128]{0:T(128)S(1)} %get-tuple-element.669, ...), kind=kLoop, calls=%fused_computation.77.clone.1 | loop fusion | flops 3670016 | bytes 2635268 | tf_op jit(solution)/shard_map/convert.2
  82.5 3.2 %fusion.196 = (bf16[128,1024]{1,0:T(8,128)(2,1)S(1)}, bf16[128,1024]{1,0:T(8,128)(2,1)S(1)}, f32[128,1024]{1,0:T(8,128)S(1)}, f32[128,1024]{1,0:T(8,128)S(1)}) fusion(f32[1024]{0:T(1024)S(1)} %bitcast.233, f32[128]{0:T(128)S(1)} %get-tuple-element.667, f32[1024]{0:T(1024)S(1)} %bitcast.235, f32[128]{0:T(128)S(1)} %get-tuple-element.669, ...), kind=kLoop, calls=%fused_computation.77.clone.1 | loop fusion | flops 3670016 | bytes 2635268 | tf_op jit(solution)/shard_map/convert.2
  86.8 3.2 %fusion.196 = (bf16[128,1024]{1,0:T(8,128)(2,1)S(1)}, bf16[128,1024]{1,0:T(8,128)(2,1)S(1)}, f32[128,1024]{1,0:T(8,128)S(1)}, f32[128,1024]{1,0:T(8,128)S(1)}) fusion(f32[1024]{0:T(1024)S(1)} %bitcast.233, f32[128]{0:T(128)S(1)} %get-tuple-element.667, f32[1024]{0:T(1024)S(1)} %bitcast.235, f32[128]{0:T(128)S(1)} %get-tuple-element.669, ...), kind=kLoop, calls=%fused_computation.77.clone.1 | loop fusion | flops 3670016 | bytes 2635268 | tf_op jit(solution)/shard_map/convert.2
  90.8 2.6 %collective-permute-start.4 = (f32[3,1024]{1,0:T(4,128)S(1)}, f32[3,1024]{1,0:T(4,128)S(1)}, u32[]{:S(2)}, u32[]{:S(2)}) collective-permute-start(f32[3,1024]{1,0:T(4,128)S(1)} %get-tuple-element.168), channel_id=1, source_target_pairs={{0,12},{4,0},{8,4},{12,8},{1,13},{5,1},{9,5},{13,9},{2,14},{6,2},{... | collective-permute-start | bytes 36872 | tf_op jit(solution)/shard_map/ppermute | solution.py:14
  94.0 0.5 maximum_maximum_fusion.4
  94.6 34.4 %while.47 = (s32[]{:T(128)}, f32[3,1024]{1,0:T(4,128)S(1)}, f32[8,3,128]{2,1,0:T(4,128)S(1)}, f32[8,128,64]{1,2,0:T(8,128)S(1)}, f32[]{:T(128)}, /*index=5*/bf16...) while((s32[]{:T(128)}, f32[3,1024]{1,0:T(4,128)S(1)}, ...), condition=%wide.region_24.25_spmd.clone, body=%wide.region_17.24_spmd.clone.sunk | while | flops 106967936 | bytes 6464403 | solution.py:114
  94.9 3.2 %fusion.207 = (bf16[128,1024]{1,0:T(8,128)(2,1)S(1)}, bf16[128,1024]{1,0:T(8,128)(2,1)S(1)}, f32[128,1024]{1,0:T(8,128)S(1)}, f32[128,1024]{1,0:T(8,128)S(1)}) fusion(f32[1024]{0:T(1024)S(1)} %bitcast.237, f32[128]{0:T(128)S(1)} %get-tuple-element.693, f32[1024]{0:T(1024)S(1)} %bitcast.239, f32[128]{0:T(128)S(1)} %get-tuple-element.695, ...), kind=kLoop, calls=%fused_computation.129.clone.1 | loop fusion | flops 3670016 | bytes 2635268 | tf_op jit(solution)/shard_map/convert.4
  99.2 3.2 %fusion.207 = (bf16[128,1024]{1,0:T(8,128)(2,1)S(1)}, bf16[128,1024]{1,0:T(8,128)(2,1)S(1)}, f32[128,1024]{1,0:T(8,128)S(1)}, f32[128,1024]{1,0:T(8,128)S(1)}) fusion(f32[1024]{0:T(1024)S(1)} %bitcast.237, f32[128]{0:T(128)S(1)} %get-tuple-element.693, f32[1024]{0:T(1024)S(1)} %bitcast.239, f32[128]{0:T(128)S(1)} %get-tuple-element.695, ...), kind=kLoop, calls=%fused_computation.129.clone.1 | loop fusion | flops 3670016 | bytes 2635268 | tf_op jit(solution)/shard_map/convert.4
  103.5 3.2 %fusion.207 = (bf16[128,1024]{1,0:T(8,128)(2,1)S(1)}, bf16[128,1024]{1,0:T(8,128)(2,1)S(1)}, f32[128,1024]{1,0:T(8,128)S(1)}, f32[128,1024]{1,0:T(8,128)S(1)}) fusion(f32[1024]{0:T(1024)S(1)} %bitcast.237, f32[128]{0:T(128)S(1)} %get-tuple-element.693, f32[1024]{0:T(1024)S(1)} %bitcast.239, f32[128]{0:T(128)S(1)} %get-tuple-element.695, ...), kind=kLoop, calls=%fused_computation.129.clone.1 | loop fusion | flops 3670016 | bytes 2635268 | tf_op jit(solution)/shard_map/convert.4
  107.8 3.2 %fusion.207 = (bf16[128,1024]{1,0:T(8,128)(2,1)S(1)}, bf16[128,1024]{1,0:T(8,128)(2,1)S(1)}, f32[128,1024]{1,0:T(8,128)S(1)}, f32[128,1024]{1,0:T(8,128)S(1)}) fusion(f32[1024]{0:T(1024)S(1)} %bitcast.237, f32[128]{0:T(128)S(1)} %get-tuple-element.693, f32[1024]{0:T(1024)S(1)} %bitcast.239, f32[128]{0:T(128)S(1)} %get-tuple-element.695, ...), kind=kLoop, calls=%fused_computation.129.clone.1 | loop fusion | flops 3670016 | bytes 2635268 | tf_op jit(solution)/shard_map/convert.4
  112.2 3.2 %fusion.207 = (bf16[128,1024]{1,0:T(8,128)(2,1)S(1)}, bf16[128,1024]{1,0:T(8,128)(2,1)S(1)}, f32[128,1024]{1,0:T(8,128)S(1)}, f32[128,1024]{1,0:T(8,128)S(1)}) fusion(f32[1024]{0:T(1024)S(1)} %bitcast.237, f32[128]{0:T(128)S(1)} %get-tuple-element.693, f32[1024]{0:T(1024)S(1)} %bitcast.239, f32[128]{0:T(128)S(1)} %get-tuple-element.695, ...), kind=kLoop, calls=%fused_computation.129.clone.1 | loop fusion | flops 3670016 | bytes 2635268 | tf_op jit(solution)/shard_map/convert.4
  116.5 3.2 %fusion.207 = (bf16[128,1024]{1,0:T(8,128)(2,1)S(1)}, bf16[128,1024]{1,0:T(8,128)(2,1)S(1)}, f32[128,1024]{1,0:T(8,128)S(1)}, f32[128,1024]{1,0:T(8,128)S(1)}) fusion(f32[1024]{0:T(1024)S(1)} %bitcast.237, f32[128]{0:T(128)S(1)} %get-tuple-element.693, f32[1024]{0:T(1024)S(1)} %bitcast.239, f32[128]{0:T(128)S(1)} %get-tuple-element.695, ...), kind=kLoop, calls=%fused_computation.129.clone.1 | loop fusion | flops 3670016 | bytes 2635268 | tf_op jit(solution)/shard_map/convert.4
  120.8 3.2 %fusion.207 = (bf16[128,1024]{1,0:T(8,128)(2,1)S(1)}, bf16[128,1024]{1,0:T(8,128)(2,1)S(1)}, f32[128,1024]{1,0:T(8,128)S(1)}, f32[128,1024]{1,0:T(8,128)S(1)}) fusion(f32[1024]{0:T(1024)S(1)} %bitcast.237, f32[128]{0:T(128)S(1)} %get-tuple-element.693, f32[1024]{0:T(1024)S(1)} %bitcast.239, f32[128]{0:T(128)S(1)} %get-tuple-element.695, ...), kind=kLoop, calls=%fused_computation.129.clone.1 | loop fusion | flops 3670016 | bytes 2635268 | tf_op jit(solution)/shard_map/convert.4
  125.1 3.2 %fusion.207 = (bf16[128,1024]{1,0:T(8,128)(2,1)S(1)}, bf16[128,1024]{1,0:T(8,128)(2,1)S(1)}, f32[128,1024]{1,0:T(8,128)S(1)}, f32[128,1024]{1,0:T(8,128)S(1)}) fusion(f32[1024]{0:T(1024)S(1)} %bitcast.237, f32[128]{0:T(128)S(1)} %get-tuple-element.693, f32[1024]{0:T(1024)S(1)} %bitcast.239, f32[128]{0:T(128)S(1)} %get-tuple-element.695, ...), kind=kLoop, calls=%fused_computation.129.clone.1 | loop fusion | flops 3670016 | bytes 2635268 | tf_op jit(solution)/shard_map/convert.4
  128.6 0.4 fusion.208
  130.3 0.6 collective-permute-start.5
  130.9 13.6 %all-gather = f32[8,32,32]{2,1,0:T(8,128)S(1)} all-gather(f32[2,32,32]{2,1,0:T(8,128)S(1)} %copy.12), channel_id=2, replica_groups=mesh['case'=2,'blk'=4,'freq'=4] {'blk'}, dimensions={0}, use_global_device_ids=true | all-gather | bytes 40960 | tf_op jit(solution)/shard_map/all_gather | solution.py:139
  144.6 1.0 copy.15
  145.7 0.7 copy.14
  146.4 20.6 %reduce-scatter.4.cloned.1.call-done = f32[256,3]{1,0:T(8,128)} async-done(((f32[1024,3]{1,0:T(8,128)}), f32[256,3]{1,0:T(8,128)}) %reduce-scatter.4.cloned.1.call-update) | async-done | bytes 3088
  167.0 1.6 copy.16
  (235 shorter events, 27.7 us)
Async XLA Ops:
  7.2 159.8 %reduce-scatter.4.cloned.1.call-start = ((), (), s32[]{:S(2)}) async-start(), calls=%async_computation.1 | async-start | bytes 655360
  7.2 46.3 %collective-permute-start.1 = (bf16[1024,128]{1,0:T(8,128)(2,1)}, bf16[1024,128]{1,0:T(8,128)(2,1)S(1)}, u32[]{:S(2)}, u32[]{:S(2)}) collective-permute-start(bf16[1024,128]{1,0:T(8,128)(2,1)} %bitcast.220), channel_id=1, source_target_pairs={{0,4},{4,8},{8,12},{12,0},{1,5},{5,9},{9,13},{13,1},{2,6},{6,10},{... | collective-permute-start | bytes 786440 | tf_op jit(solution)/shard_map/ppermute | solution.py:14
  10.3 8.7 %collective-permute-start = (bf16[3,1024]{1,0:T(4,128)(2,1)}, bf16[3,1024]{1,0:T(4,128)(2,1)S(1)}, u32[]{:S(2)}, u32[]{:S(2)}) collective-permute-start(bf16[3,1024]{1,0:T(4,128)(2,1)} %param.10), channel_id=1, source_target_pairs={{0,4},{4,8},{8,12},{12,0},{1,5},{5,9},{9,13},{13,1},{2,6},{6,10},{... | collective-permute-start | bytes 18440 | tf_op jit(solution)/shard_map/ppermute | solution.py:14
  11.9 1.7 copy-start
  13.7 0.7 copy-start.2
  13.7 0.7 copy-start.3
  14.8 1.2 copy-start.1
  19.0 34.5 %collective-permute-start.2 = (bf16[3,1024]{1,0:T(4,128)(2,1)S(1)}, bf16[3,1024]{1,0:T(4,128)(2,1)S(1)}, u32[]{:S(2)}, u32[]{:S(2)}) collective-permute-start(bf16[3,1024]{1,0:T(4,128)(2,1)S(1)} %collective-permute-done), channel_id=1, source_target_pairs={{0,4},{4,8},{8,12},{12,0},{1,5},{5,9},{9,13},{13,1},{2,6},{6,10},{... | collective-permute-start | bytes 18440 | tf_op jit(solution)/shard_map/ppermute | solution.py:14
  54.7 38.7 %collective-permute-start.3 = (bf16[1024,128]{1,0:T(8,128)(2,1)S(1)}, bf16[1024,128]{1,0:T(8,128)(2,1)S(1)}, u32[]{:S(2)}, u32[]{:S(2)}) collective-permute-start(bf16[1024,128]{1,0:T(8,128)(2,1)S(1)} %collective-permute-done.1), channel_id=1, source_target_pairs={{0,4},{4,8},{8,12},{12,0},{1,5},{5,9},{9,13},{13,1},{2,6},{6,10},{... | collective-permute-start | bytes 786440 | tf_op jit(solution)/shard_map/ppermute | solution.py:14
  90.8 53.8 %collective-permute-start.4 = (f32[3,1024]{1,0:T(4,128)S(1)}, f32[3,1024]{1,0:T(4,128)S(1)}, u32[]{:S(2)}, u32[]{:S(2)}) collective-permute-start(f32[3,1024]{1,0:T(4,128)S(1)} %get-tuple-element.168), channel_id=1, source_target_pairs={{0,12},{4,0},{8,4},{12,8},{1,13},{5,1},{9,5},{13,9},{2,14},{6,2},{... | collective-permute-start | bytes 36872 | tf_op jit(solution)/shard_map/ppermute | solution.py:14
  130.3 14.3 %collective-permute-start.5 = (f32[3,1024]{1,0:T(4,128)S(1)}, f32[3,1024]{1,0:T(4,128)S(1)}, u32[]{:S(2)}, u32[]{:S(2)}) collective-permute-start(f32[3,1024]{1,0:T(4,128)S(1)} %get-tuple-element.169), channel_id=1, source_target_pairs={{0,8},{4,12},{8,0},{12,4},{1,9},{5,13},{9,1},{13,5},{2,10},{6,14},... | collective-permute-start | bytes 36872 | tf_op jit(solution)/shard_map/ppermute | solution.py:14
Sparse Core Ops, SparseCore 0:
  145.8 21.1 reduce-scatter.3
